TPU v7x, 32 devices: a whole 2x2x4 slice. The times are simulated.
32 devices in a mesh: dp: 16 (over z, x, core), mp: 2 (over y).
Axes of the slice: x: 2, y: 2, z: 4, core: 2. Of those that a mesh axis runs over, the one named last changes fastest.
Arguments:
- tokens: bfloat16 [16384, 1024], P('dp'), may hold values from -6 to 6
- page_lengths: int32 [32], P('dp'), may hold values from 64 to 512, as said below
- qkv_weight: bfloat16 [3, 1024, 1024], P(None, None, 'mp'), may hold values from -0.1875 to 0.1875
- qv_bias: bfloat16 [2, 1024], P(None, 'mp'), may hold values from -1.5 to 1.5
- out_weight: bfloat16 [1024, 1024], P('mp'), may hold values from -0.75 to 0.75
- out_bias: bfloat16 [1024], replicated, may hold values from -1.5 to 1.5
- ln1_gain: bfloat16 [1024], replicated, may hold values from 0.5 to 1.5
- ln1_bias: bfloat16 [1024], replicated, may hold values from -1.5 to 1.5
- ff1_weight: bfloat16 [1024, 4096], P(None, 'mp'), may hold values from -0.1875 to 0.1875
- ff1_bias: bfloat16 [4096], P('mp'), may hold values from -1.5 to 1.5
- ff2_weight: bfloat16 [4096, 1024], P('mp'), may hold values from -0.09375 to 0.09375
- ff2_bias: bfloat16 [1024], replicated, may hold values from -1.5 to 1.5
- ln2_gain: bfloat16 [1024], replicated, may hold values from 0.5 to 1.5
- ln2_bias: bfloat16 [1024], replicated, may hold values from -1.5 to 1.5
- cotangent: bfloat16 [16384, 1024], P('dp'), may hold values from -6 to 6
Outputs:
- out_rows: bfloat16 [16384, 1024], P(('dp', 'mp'))
- input_grad: bfloat16 [16384, 1024], P(('dp', 'mp'))
- qkv_weight_grad: float32 [3, 1024, 1024], P(None, 'dp', 'mp')
- qv_bias_grad: float32 [2, 1024], replicated
- out_weight_grad: float32 [1024, 1024], P('mp', 'dp')
- out_bias_grad: float32 [1024], replicated
- ln1_gain_grad: float32 [1024], replicated
- ln1_bias_grad: float32 [1024], replicated
- ff1_weight_grad: float32 [1024, 4096], P('dp', 'mp')
- ff1_bias_grad: float32 [4096], replicated
- ff2_weight_grad: float32 [4096, 1024], P('mp', 'dp')
- ff2_bias_grad: float32 [1024], replicated
- ln2_gain_grad: float32 [1024], replicated
- ln2_bias_grad: float32 [1024], replicated
Inputs may be any that keep to these rules, and one draw needn't show every extreme that they name: `page_lengths`: valid tokens of a page; some page has all 512 slots valid.
All inputs are finite; a program needn't handle non-finite values.
Results may differ from a plain program's by a relative error of at most 0.02.
Values may be sent and summed in bfloat16 or wider, within the bound.
No kernel may reach another device: no remote copies, remote signals or barrier semaphores. Data moves between devices by JAX's collectives and lax.ppermute only.
A program may use at most 192 MiB of HBM per device.

v0:
```python
import jax
import jax.numpy as jnp
from jax import lax
from jax.sharding import PartitionSpec as P

HD = 64
EPSILON = 1e-05
NEGATIVE = -1e30


def normalize(values):
    center = values - jnp.mean(values, axis=-1, keepdims=True)
    spread = jnp.mean(center * center, axis=-1, keepdims=True)
    return center * lax.rsqrt(spread + EPSILON)


def gelu_exact(values):
    return jax.nn.gelu(values, approximate=False)


def over_rows(left, right):
    return lax.dot_general(
        left, right, (((0,), (0,)), ((), ())), preferred_element_type=jnp.float32
    )


def over_cols(left, right):
    return lax.dot_general(
        left, right, (((1,), (1,)), ((), ())), preferred_element_type=jnp.float32
    )


def page_scores(query, keyset, valid):
    raw = jnp.einsum("qhe,khe->hqk", query, keyset, preferred_element_type=jnp.float32) * HD ** (
        -0.5
    )
    return jnp.where(valid[None, None, :], raw, NEGATIVE)


def attend(block):
    query, keyset, valueset, valid = block
    scores = page_scores(query, keyset, valid)
    top = jnp.max(scores, axis=-1, keepdims=True)
    expo = jnp.exp(scores - top)
    total = jnp.sum(expo, axis=-1, keepdims=True)
    probs = expo / total
    context = jnp.einsum(
        "hqk,khe->qhe", probs.astype(jnp.bfloat16), valueset, preferred_element_type=jnp.float32
    )
    context = context.astype(jnp.bfloat16)
    return (context.reshape(context.shape[0], -1), top[..., 0] + jnp.log(total[..., 0]))


def attend_back(block):
    query, keyset, valueset, valid, logsum, dcontext = block
    scale = HD ** (-0.5)
    scores = page_scores(query, keyset, valid)
    probs = jnp.exp(scores - logsum[..., None])
    dprobs = jnp.einsum("qhe,khe->hqk", dcontext, valueset, preferred_element_type=jnp.float32)
    delta = jnp.sum(probs * dprobs, axis=-1, keepdims=True)
    dscores = (probs * (dprobs - delta)).astype(jnp.bfloat16)
    dquery = (
        jnp.einsum("hqk,khe->qhe", dscores, keyset, preferred_element_type=jnp.float32) * scale
    ).astype(jnp.bfloat16)
    dkeys = (
        jnp.einsum("hqk,qhe->khe", dscores, query, preferred_element_type=jnp.float32) * scale
    ).astype(jnp.bfloat16)
    dvalues = jnp.einsum(
        "hqk,qhe->khe", probs.astype(jnp.bfloat16), dcontext, preferred_element_type=jnp.float32
    ).astype(jnp.bfloat16)
    seq_len = query.shape[0]
    return (dquery.reshape(seq_len, -1), dkeys.reshape(seq_len, -1), dvalues.reshape(seq_len, -1))


def local(
    tokens,
    page_lengths,
    qkv_weight,
    qv_bias,
    out_weight,
    out_bias,
    ln1_gain,
    ln1_bias,
    ff1_weight,
    ff1_bias,
    ff2_weight,
    ff2_bias,
    ln2_gain,
    ln2_bias,
    cotangent,
):
    row_count = tokens.shape[0]
    page_count = page_lengths.shape[0]
    seq_len = row_count // page_count
    cols = qkv_weight.shape[2]
    ff_cols = ff1_weight.shape[1]
    group_heads = cols // HD
    share = row_count // lax.axis_size("mp")
    group = lax.axis_index("mp")
    share_start = group * share
    gain_one = ln1_gain.astype(jnp.float32)
    shift_one = ln1_bias.astype(jnp.float32)
    gain_two = ln2_gain.astype(jnp.float32)
    shift_two = ln2_bias.astype(jnp.float32)

    def own_rows(values):
        return lax.dynamic_slice_in_dim(values, share_start, share, 0)

    projected = jnp.einsum("rd,tdc->trc", tokens, qkv_weight, preferred_element_type=jnp.float32)
    bias_rows = jnp.stack([qv_bias[0], jnp.zeros_like(qv_bias[0]), qv_bias[1]]).astype(jnp.float32)
    qkv_rows = (projected + bias_rows[:, None, :]).astype(jnp.bfloat16)
    qkv_pages = qkv_rows.reshape(3, page_count, seq_len, group_heads, HD)
    valid = jnp.arange(seq_len)[None, :] < page_lengths[:, None]
    context, logsum = lax.map(attend, (qkv_pages[0], qkv_pages[1], qkv_pages[2], valid))
    context = context.reshape(row_count, cols)
    attn_part = jnp.dot(context, out_weight, preferred_element_type=jnp.float32).astype(
        jnp.bfloat16
    )
    attn = lax.psum(attn_part, "mp").astype(jnp.float32)
    first_sum = tokens.astype(jnp.float32) + attn + out_bias.astype(jnp.float32)
    normed_one, norm_one_back = jax.vjp(normalize, first_sum)
    hidden = normed_one * gain_one + shift_one
    hidden_low = hidden.astype(jnp.bfloat16)
    normed_one_own = own_rows(normed_one)
    pre = jnp.dot(hidden_low, ff1_weight, preferred_element_type=jnp.float32) + ff1_bias.astype(
        jnp.float32
    )
    activated, gelu_back = jax.vjp(gelu_exact, pre)
    act_low = activated.astype(jnp.bfloat16)
    ffn_part = jnp.dot(act_low, ff2_weight, preferred_element_type=jnp.float32).astype(jnp.bfloat16)
    cot_own = own_rows(cotangent).astype(jnp.float32)
    ffn = lax.psum(ffn_part, "mp").astype(jnp.float32)
    second_sum = hidden + ffn + ff2_bias.astype(jnp.float32)
    normed_two, norm_two_back = jax.vjp(normalize, second_sum)
    normed_two_own = own_rows(normed_two)
    out_rows = (normed_two_own * gain_two + shift_two).astype(jnp.bfloat16)
    dsecond = norm_two_back(cotangent.astype(jnp.float32) * gain_two)[0]
    dffn = dsecond.astype(jnp.bfloat16)
    dsecond_own = own_rows(dsecond)
    dgain_two = jnp.sum(cot_own * normed_two_own, axis=0)
    dshift_two = jnp.sum(cot_own, axis=0)
    dff2_bias = jnp.sum(dsecond_own, axis=0)
    dff2_weight = over_rows(act_low, dffn)
    dact = over_cols(dffn, ff2_weight)
    dpre = gelu_back(dact)[0].astype(jnp.bfloat16)
    dff1_bias = jnp.sum(dpre.astype(jnp.float32), axis=0)
    dff1_weight = over_rows(hidden_low, dpre)
    dhid_part = over_cols(dpre, ff1_weight).astype(jnp.bfloat16)
    dhidden = dsecond + lax.psum(dhid_part, "mp").astype(jnp.float32)
    dfirst = norm_one_back(dhidden * gain_one)[0]
    dattn = dfirst.astype(jnp.bfloat16)
    dhidden_own = own_rows(dhidden)
    dfirst_own = own_rows(dfirst)
    dgain_one = jnp.sum(dhidden_own * normed_one_own, axis=0)
    dshift_one = jnp.sum(dhidden_own, axis=0)
    dout_bias = jnp.sum(dfirst_own, axis=0)
    dout_weight = over_rows(context, dattn)
    dcontext = over_cols(dattn, out_weight).astype(jnp.bfloat16)
    dcontext_pages = dcontext.reshape(page_count, seq_len, group_heads, HD)
    dquery, dkeys, dvalues = lax.map(
        attend_back, (qkv_pages[0], qkv_pages[1], qkv_pages[2], valid, logsum, dcontext_pages)
    )
    dqkv = jnp.stack(
        [
            dquery.reshape(row_count, cols),
            dkeys.reshape(row_count, cols),
            dvalues.reshape(row_count, cols),
        ]
    )
    dqv_bias = jnp.stack(
        [jnp.sum(dqkv[0].astype(jnp.float32), axis=0), jnp.sum(dqkv[2].astype(jnp.float32), axis=0)]
    )
    dqkv_weight = jnp.einsum("rd,trc->tdc", tokens, dqkv, preferred_element_type=jnp.float32)
    dtok_part = jnp.einsum(
        "trc,tdc->rd", dqkv, qkv_weight, preferred_element_type=jnp.float32
    ).astype(jnp.bfloat16)
    input_grad = (
        dfirst_own
        + lax.psum_scatter(dtok_part, "mp", scatter_dimension=0, tiled=True).astype(jnp.float32)
    ).astype(jnp.bfloat16)
    qkv_share, out_share, ff1_share, ff2_share = (
        lax.psum_scatter(
            dqkv_weight.astype(jnp.bfloat16), "dp", scatter_dimension=1, tiled=True
        ).astype(jnp.float32),
        lax.psum_scatter(
            dout_weight.astype(jnp.bfloat16), "dp", scatter_dimension=1, tiled=True
        ).astype(jnp.float32),
        lax.psum_scatter(
            dff1_weight.astype(jnp.bfloat16), "dp", scatter_dimension=0, tiled=True
        ).astype(jnp.float32),
        lax.psum_scatter(
            dff2_weight.astype(jnp.bfloat16), "dp", scatter_dimension=1, tiled=True
        ).astype(jnp.float32),
    )
    qv_placed = lax.dynamic_update_slice_in_dim(
        jnp.zeros((2, cols * lax.axis_size("mp")), jnp.float32), dqv_bias, group * cols, 1
    )
    ff1_placed = lax.dynamic_update_slice_in_dim(
        jnp.zeros((ff_cols * lax.axis_size("mp"),), jnp.float32), dff1_bias, group * ff_cols, 0
    )
    small = lax.psum(
        (qv_placed, dout_bias, dgain_one, dshift_one, ff1_placed, dff2_bias, dgain_two, dshift_two),
        ("dp", "mp"),
    )
    return (
        out_rows,
        input_grad,
        qkv_share,
        small[0],
        out_share,
        small[1],
        small[2],
        small[3],
        ff1_share,
        small[4],
        ff2_share,
        small[5],
        small[6],
        small[7],
    )


def solution(mesh):
    in_specs = (
        P("dp", None),
        P("dp"),
        P(None, None, "mp"),
        P(None, "mp"),
        P("mp", None),
        P(),
        P(),
        P(),
        P(None, "mp"),
        P("mp"),
        P("mp", None),
        P(),
        P(),
        P(),
        P("dp", None),
    )
    out_specs = (
        P(("dp", "mp"), None),
        P(("dp", "mp"), None),
        P(None, "dp", "mp"),
        P(),
        P("mp", "dp"),
        P(),
        P(),
        P(),
        P("dp", "mp"),
        P(),
        P("mp", "dp"),
        P(),
        P(),
        P(),
    )
    return jax.shard_map(local, mesh=mesh, in_specs=in_specs, out_specs=out_specs, check_vma=False)
```

profile of v0, /device:TPU:0, one launch (start us, length us, event | category | flops | bytes accessed | tf_op | source)
XLA Modules:
  0.0 775.8 jit_solution(8002461027185806768)
XLA Ops:
  9.1 5.5 fusion.56
  32.4 24.3 %while.26 = (s32[]{:T(128)}, bf16[2,512,512]{2,1,0:T(8,128)(2,1)}, f32[2,8,512]{2,1,0:T(8,128)S(1)}, bf16[2,512,8,64]{1,3,2,0:T(8,128)(2,1)}, pred[2,512]{1,0:T(...) while((s32[]{:T(128)}, bf16[2,512,512]{2,1,0:T(8,128)(2,1)}, ...), condition=%wide.region_3.4_spmd, body=%wide.region_0.3_spmd.sunk | while | flops 562294784 | bytes 33689224 | solution.py:114
  56.7 4.2 convolution_convert_fusion.4
  61.3 65.4 %all-reduce.7.cloned.1.call-done = bf16[1024,1024]{1,0:T(8,128)(2,1)} async-done(((bf16[1024,1024]{1,0:T(8,128)(2,1)}), bf16[1024,1024]{1,0:T(8,128)(2,1)}) %all-reduce.7.cloned.1.call-update) | async-done | bytes 2097168 | tf_op jit(solution)/shard_map/psum | solution.py:119
  133.5 24.4 %multiply_convert_fusion.1 = (bf16[1024,2048]{1,0:T(8,128)(2,1)S(1)}, f32[1024,2048]{1,0:T(8,128)}, f32[1024,2048]{1,0:T(8,128)}) fusion(f32[2048]{0:T(1024)S(1)} %convert_element_type.172, bf16[1024,2048]{1,0:T(8,128)(2,1)S(1)} %copy-done.36, f32[1024,1024]{1,0:T(8,128)S(1)} %broadcast_multiply_fusion, f32[1024]{0:T(1024)S(1)} %convert_element_type.170, ...), kind=kOutput, calls=%fused_computation.64 | convolution fusion | flops 4436525056 | bytes 29376512 | tf_op jit(solution)/shard_map/dot_general | solution.py:125
  159.9 5.7 convolution_convert_fusion.3
  166.2 62.6 %all-reduce.9.cloned.1.call-done = bf16[1024,1024]{1,0:T(8,128)(2,1)} async-done(((bf16[1024,1024]{1,0:T(8,128)(2,1)}), bf16[1024,1024]{1,0:T(8,128)(2,1)}) %all-reduce.9.cloned.1.call-update) | async-done | bytes 2097168 | tf_op jit(solution)/shard_map/psum | solution.py:132
  241.1 13.0 %convert_reduce_fusion = (f32[2048]{0:T(1024)}, bf16[1024,2048]{1,0:T(8,128)(2,1)}) fusion(f32[1024,2048]{1,0:T(8,128)} %get-tuple-element.258, bf16[2048,1024]{1,0:T(8,128)(2,1)S(1)} %copy-done.35, f32[1024,1024]{1,0:T(8,128)S(1)} %broadcast_add_fusion.1, f32[1024,2048]{1,0:T(8,128)} %get-tuple-element.275, f32[2048]{0:T(1024)S(1)} %convert_element_type.172), kind=kOutput, calls=%fused_computation.62 | convolution fusion | flops 4331665408 | bytes 29376512 | tf_op jit(solution)/shard_map/dot_general | solution.py:28
  254.1 8.0 %convolution_convert_fusion.2 = bf16[1024,1024]{1,0:T(8,128)(2,1)} fusion(bf16[1024,2048]{1,0:T(8,128)(2,1)} %get-tuple-element.277, bf16[1024,2048]{1,0:T(8,128)(2,1)S(1)} %copy-done.37), kind=kOutput, calls=%fused_computation.118 | convolution fusion | flops 4296015872 | bytes 10485760 | tf_op jit(solution)/shard_map/dot_general | solution.py:28
  262.2 63.0 %all-reduce.11.cloned.1.call-done = bf16[1024,1024]{1,0:T(8,128)(2,1)} async-done(((bf16[1024,1024]{1,0:T(8,128)(2,1)}), bf16[1024,1024]{1,0:T(8,128)(2,1)}) %all-reduce.11.cloned.1.call-update) | async-done | bytes 2097168 | tf_op jit(solution)/shard_map/psum | solution.py:149
  325.2 5.7 multiply_reduce_fusion.1
  346.2 42.9 %while.27 = (s32[]{:T(128)}, bf16[2,512,512]{1,2,0:T(8,128)(2,1)}, bf16[2,512,512]{2,1,0:T(8,128)(2,1)}, bf16[2,512,512]{1,2,0:T(8,128)(2,1)}, bf16[2,512,8,64]{...) while((s32[]{:T(128)}, bf16[2,512,512]{1,2,0:T(8,128)(2,1)}, ...), condition=%wide.region_17.18_spmd, body=%wide.region_15.17_spmd.sunk | while | flops 1374941184 | bytes 89248512 | solution.py:160
  393.7 7.7 convert_bitcast_fusion
  401.4 7.7 copy.83
  409.1 4.8 convolution_convert_fusion.5
  414.0 10.2 %convolution_convert_fusion = bf16[2048,1024]{0,1:T(8,128)(2,1)} fusion(bf16[1024,2048]{1,0:T(8,128)(2,1)} %copy-done.40, f32[1024,1024]{1,0:T(8,128)} %copy-done.11), kind=kOutput, calls=%fused_computation.91 | convolution fusion | flops 4298113024 | bytes 12582912 | tf_op jit(solution)/shard_map/dot_general | solution.py:22
  424.3 6.6 bitcast_convert_fusion
  431.3 10.2 %convolution_convert_fusion.1 = bf16[1024,2048]{1,0:T(8,128)(2,1)} fusion(bf16[1024,2048]{1,0:T(8,128)(2,1)} %get-tuple-element.277, f32[1024,1024]{1,0:T(8,128)} %copy-done.7, f32[1024]{0:T(1024)S(1)} %copy-done.25, f32[1024]{0:T(1024)S(1)} %convert_element_type.169), kind=kOutput, calls=%fused_computation.92 | convolution fusion | flops 4300210176 | bytes 12591104 | tf_op jit(solution)/shard_map/dot_general | solution.py:22
  452.0 68.8 %all-reduce.13.cloned.1.call-done = bf16[3,1024,512]{2,0,1:T(4,128)(2,1)} async-done(((bf16[3,1024,512]{2,0,1:T(4,128)(2,1)}), bf16[3,1024,512]{2,0,1:T(4,128)(2,1)}) %all-reduce.13.cloned.1.call-update) | async-done | bytes 3145744
  522.7 57.9 %reduce-scatter.7.cloned.1.call-done = bf16[512,64]{0,1:T(8,128)(2,1)} async-done(((bf16[512,1024]{0,1:T(8,128)(2,1)}), bf16[512,64]{0,1:T(8,128)(2,1)}) %reduce-scatter.7.cloned.1.call-update) | async-done | bytes 65552 | tf_op jit(solution)/shard_map/reduce_scatter | solution.py:185
  582.1 74.2 %reduce-scatter.11.cloned.1.call-done = bf16[2048,64]{0,1:T(8,128)(2,1)} async-done(((bf16[2048,1024]{0,1:T(8,128)(2,1)}), bf16[2048,64]{0,1:T(8,128)(2,1)}) %reduce-scatter.11.cloned.1.call-update) | async-done | bytes 262160 | tf_op jit(solution)/shard_map/reduce_scatter | solution.py:191
  658.1 31.3 %reduce-scatter.5.cloned.1.call-done = bf16[512,1024]{1,0:T(8,128)(2,1)} async-done(((bf16[1024,1024]{1,0:T(8,128)(2,1)}), bf16[512,1024]{1,0:T(8,128)(2,1)}) %reduce-scatter.5.cloned.1.call-update) | async-done | bytes 1048592 | tf_op jit(solution)/shard_map/reduce_scatter | solution.py:179
  692.6 40.9 %all-reduce.1 = (f32[2,1024]{1,0:T(2,128)}, f32[1024]{0:T(1024)}, f32[1024]{0:T(1024)}, f32[1024]{0:T(1024)}, f32[4096]{0:T(1024)}, /*index=5*/f32[1024]{0:T(1024)}, f32[1024]{0:T(1024)}, f32[1024]{0:T(1024)}) all-reduce(f32[2,1024]{1,0:T(2,128)S(1)} %maximum_dynamic-update-slice_fusion, ...), channel_id=1, replica_groups=mesh['dp'=16,'mp'=2] {'dp','mp'}, use_global_device_ids=true, to_apply=%region_22.23 | all-reduce | flops 12288 | bytes 98304 | tf_op jit(solution)/shard_map/psum | solution.py:201
  733.5 33.2 %reduce-scatter.9.cloned.1.call-done = bf16[64,2048]{1,0:T(8,128)(2,1)} async-done(((bf16[1024,2048]{1,0:T(8,128)(2,1)}), bf16[64,2048]{1,0:T(8,128)(2,1)}) %reduce-scatter.9.cloned.1.call-update) | async-done | bytes 262160 | tf_op jit(solution)/shard_map/reduce_scatter | solution.py:188
  (204 shorter events, 148.5 us)
Async XLA Ops:
  7.2 119.5 %all-reduce.7.cloned.1.call-start = ((), (), s32[]{:S(2)}) async-start(), calls=%async_computation.4 | async-start | bytes 4194304 | tf_op jit(solution)/shard_map/psum | solution.py:119
  56.7 4.6 copy-start.27
  60.9 167.8 %all-reduce.9.cloned.1.call-start = ((), (), s32[]{:S(2)}) async-start(), calls=%async_computation.5 | async-start | bytes 4194304 | tf_op jit(solution)/shard_map/psum | solution.py:132
  61.3 171.4 %copy-start.24 = (f32[1024]{0:T(1024)}, f32[1024]{0:T(1024)S(1)}, u32[]{:S(2)}) copy-start(f32[1024]{0:T(1024)S(1)} %convert_element_type.170) | copy-start | bytes 12292
  133.4 24.4 %copy-start.7 = (f32[1024,1024]{1,0:T(8,128)}, f32[1024,1024]{1,0:T(8,128)S(1)}, u32[]{:S(2)}) copy-start(f32[1024,1024]{1,0:T(8,128)S(1)} %broadcast_multiply_fusion) | copy-start | bytes 12582916
  133.5 26.5 %copy-start.34 = (bf16[2048,1024]{1,0:T(8,128)(2,1)S(1)}, bf16[2048,1024]{1,0:T(8,128)(2,1)}, u32[]{:S(2)}) copy-start(bf16[2048,1024]{1,0:T(8,128)(2,1)} %param.29) | copy-start | bytes 12582916
  159.9 6.2 copy-start.31
  159.9 6.2 copy-start.32
  165.7 159.5 %all-reduce.11.cloned.1.call-start = ((), (), s32[]{:S(2)}) async-start(), calls=%async_computation.6 | async-start | bytes 4194304 | tf_op jit(solution)/shard_map/psum | solution.py:149
  166.2 72.0 %copy-start.20 = (f32[1024]{0:T(1024)}, f32[1024]{0:T(1024)S(1)}, u32[]{:S(2)}) copy-start(f32[1024]{0:T(1024)S(1)} %convert_element_type.177) | copy-start | bytes 12292
  228.8 4.7 copy-start.13
  239.4 14.7 %copy-start.11 = (f32[1024,1024]{1,0:T(8,128)}, f32[1024,1024]{1,0:T(8,128)S(1)}, u32[]{:S(2)}) copy-start(f32[1024,1024]{1,0:T(8,128)S(1)} %broadcast_add_fusion.1) | copy-start | bytes 12582916
  241.1 13.0 %copy-start.37 = (bf16[1024,2048]{1,0:T(8,128)(2,1)S(1)}, bf16[1024,2048]{1,0:T(8,128)(2,1)}, u32[]{:S(2)}) copy-start(bf16[1024,2048]{1,0:T(8,128)(2,1)} %param.27) | copy-start | bytes 12582916
  262.1 258.7 %all-reduce.13.cloned.1.call-start = ((), (), s32[]{:S(2)}) async-start(), calls=%async_computation.11 | async-start | bytes 8388608
  325.2 5.8 copy-start.4
  325.2 5.8 copy-start.6
  409.1 171.5 %reduce-scatter.7.cloned.1.call-start = ((), (), s32[]{:S(2)}) async-start(), calls=%async_computation.8 | async-start | bytes 1114112 | tf_op jit(solution)/shard_map/reduce_scatter | solution.py:185
  414.0 242.3 %reduce-scatter.11.cloned.1.call-start = ((), (), s32[]{:S(2)}) async-start(), calls=%async_computation.10 | async-start | bytes 4456448 | tf_op jit(solution)/shard_map/reduce_scatter | solution.py:191
  424.3 7.0 copy-start.25
  424.3 265.1 %reduce-scatter.5.cloned.1.call-start = ((), (), s32[]{:S(2)}) async-start(), calls=%async_computation.7 | async-start | bytes 3145728 | tf_op jit(solution)/shard_map/reduce_scatter | solution.py:179
  431.0 335.8 %reduce-scatter.9.cloned.1.call-start = ((), (), s32[]{:S(2)}) async-start(), calls=%async_computation.9 | async-start | bytes 4456448 | tf_op jit(solution)/shard_map/reduce_scatter | solution.py:188
  443.4 6.0 copy-start.9
  445.8 5.8 copy-start.18
  445.8 5.8 copy-start.19
  (30 other events, 79.6 us)
Sparse Core Ops, SparseCore 0:
  61.1 65.5 all-reduce.6
  165.8 62.9 all-reduce.8
  262.2 62.9 all-reduce.10
  409.2 111.5 all-reduce.12
  524.3 56.2 reduce-scatter.6
  584.8 71.4 reduce-scatter.10
  658.5 30.8 reduce-scatter.4
  693.8 72.9 reduce-scatter.8
where the time goes:
time: 785 us; the launch traced here: 776 us
  waiting for transfers between devices  457 us (58%)
  matrix products  139 us (18%)
  local copies, waits for them, and re-layouts  70.2 us (9%)
  other arithmetic  51.3 us (7%)
  blocking collectives  40.9 us (5%)
  between operations  15.7 us (2%)
    reduce_scatter x1, waiting for transfers between devices, local(): lax.psum_scatter(dff2_weight.astype(jnp.bfloat16), 'dp', scatter_dimensio...  74.2 us
    unnamed x9, waiting for transfers between devices  68.9 us
    psum x1, waiting for transfers between devices, local(): attn = lax.psum(attn_part, 'mp').astype(jnp.float32)  65.4 us
    psum x1, waiting for transfers between devices, local(): dhidden = dsecond + lax.psum(dhid_part, 'mp').astype(jnp.float32)  63 us
    psum x1, waiting for transfers between devices, local(): ffn = lax.psum(ffn_part, 'mp').astype(jnp.float32)  62.6 us
    reduce_scatter x1, waiting for transfers between devices, local(): lax.psum_scatter(dout_weight.astype(jnp.bfloat16), 'dp', scatter_dimensio...  57.9 us
    psum x1, blocking collectives, local(): lax.psum((qv_placed, dout_bias, dgain_one, dshift_one, ff1_placed, dff2_b...  40.9 us
    reduce_scatter x1, waiting for transfers between devices, local(): lax.psum_scatter(dff1_weight.astype(jnp.bfloat16), 'dp', scatter_dimensio...  33.2 us
  transfers between devices with their start and end apart: 8, of which 8 were waited for; matrix products, arithmetic and copies ran while one was open for 6% of the time, Pallas kernels for 0%

commit v1 on v0

--- a/solution.py
+++ b/solution.py
@@ -198,10 +198,11 @@
     ff1_placed = lax.dynamic_update_slice_in_dim(
         jnp.zeros((ff_cols * lax.axis_size("mp"),), jnp.float32), dff1_bias, group * ff_cols, 0
     )
-    small = lax.psum(
+    partial = lax.psum(
         (qv_placed, dout_bias, dgain_one, dshift_one, ff1_placed, dff2_bias, dgain_two, dshift_two),
-        ("dp", "mp"),
-    )
+        "dp",
+    )
+    small = lax.psum(partial, "mp")
     return (
         out_rows,
         input_grad,

time: 785 us -> 785 us (level)
  waiting for transfers between devices: 457 us -> 427 us
  blocking collectives: 40.9 us -> 70.6 us
    reduce_scatter x1, waiting for transfers between devices: 33.2 us -> 3.53 us  [local(): lax.psum_scatter(dff1_weight.astype(jnp.bfloat16), 'dp', scatter_dimensio...]
    psum x1, blocking collectives: 40.9 us -> 62.3 us  [local(): lax.psum((qv_placed, dout_bias, dgain_one, dshift_one, ff1_placed, dff2_b...]
    psum x0 -> x1, blocking collectives: none -> 8.3 us  [local(): small = lax.psum(partial, 'mp')]
where the time goes in v1:
time: 785 us; the launch traced here: 776 us
  waiting for transfers between devices  427 us (54%)
  matrix products  139 us (18%)
  blocking collectives  70.6 us (9%)
  local copies, waits for them, and re-layouts  70.2 us (9%)
  other arithmetic  51.3 us (7%)
  between operations  15.7 us (2%)
    reduce_scatter x1, waiting for transfers between devices, local(): lax.psum_scatter(dff2_weight.astype(jnp.bfloat16), 'dp', scatter_dimensio...  74.2 us
    unnamed x9, waiting for transfers between devices  68.9 us
    psum x1, waiting for transfers between devices, local(): attn = lax.psum(attn_part, 'mp').astype(jnp.float32)  65.4 us
    psum x1, waiting for transfers between devices, local(): dhidden = dsecond + lax.psum(dhid_part, 'mp').astype(jnp.float32)  63 us
    psum x1, waiting for transfers between devices, local(): ffn = lax.psum(ffn_part, 'mp').astype(jnp.float32)  62.6 us
    psum x1, blocking collectives, local(): lax.psum((qv_placed, dout_bias, dgain_one, dshift_one, ff1_placed, dff2_b...  62.3 us
    reduce_scatter x1, waiting for transfers between devices, local(): lax.psum_scatter(dout_weight.astype(jnp.bfloat16), 'dp', scatter_dimensio...  57.9 us
    reduce_scatter x1, waiting for transfers between devices, local(): lax.psum_scatter(dtok_part, 'mp', scatter_dimension=0, tiled=True)  31.3 us
  transfers between devices with their start and end apart: 8, of which 8 were waited for; matrix products, arithmetic and copies ran while one was open for 6% of the time, Pallas kernels for 0%

profile of v1, /device:TPU:0, one launch (start us, length us, event | category | flops | bytes accessed | tf_op | source)
XLA Modules:
  0.0 775.8 jit_solution(8641743296553900225)
XLA Ops:
  9.1 5.5 fusion.56
  32.4 24.3 %while.26 = (s32[]{:T(128)}, bf16[2,512,512]{2,1,0:T(8,128)(2,1)}, f32[2,8,512]{2,1,0:T(8,128)S(1)}, bf16[2,512,8,64]{1,3,2,0:T(8,128)(2,1)}, pred[2,512]{1,0:T(...) while((s32[]{:T(128)}, bf16[2,512,512]{2,1,0:T(8,128)(2,1)}, ...), condition=%wide.region_3.4_spmd, body=%wide.region_0.3_spmd.sunk | while | flops 562294784 | bytes 33689224 | solution.py:114
  56.7 4.2 convolution_convert_fusion.4
  61.3 65.4 %all-reduce.8.cloned.1.call-done = bf16[1024,1024]{1,0:T(8,128)(2,1)} async-done(((bf16[1024,1024]{1,0:T(8,128)(2,1)}), bf16[1024,1024]{1,0:T(8,128)(2,1)}) %all-reduce.8.cloned.1.call-update) | async-done | bytes 2097168 | tf_op jit(solution)/shard_map/psum | solution.py:119
  133.5 24.4 %multiply_convert_fusion.1 = (bf16[1024,2048]{1,0:T(8,128)(2,1)S(1)}, f32[1024,2048]{1,0:T(8,128)}, f32[1024,2048]{1,0:T(8,128)}) fusion(f32[2048]{0:T(1024)S(1)} %convert_element_type.172, bf16[1024,2048]{1,0:T(8,128)(2,1)S(1)} %copy-done.36, f32[1024,1024]{1,0:T(8,128)S(1)} %broadcast_multiply_fusion, f32[1024]{0:T(1024)S(1)} %convert_element_type.170, ...), kind=kOutput, calls=%fused_computation.64 | convolution fusion | flops 4436525056 | bytes 29376512 | tf_op jit(solution)/shard_map/dot_general | solution.py:125
  159.9 5.7 convolution_convert_fusion.3
  166.2 62.6 %all-reduce.10.cloned.1.call-done = bf16[1024,1024]{1,0:T(8,128)(2,1)} async-done(((bf16[1024,1024]{1,0:T(8,128)(2,1)}), bf16[1024,1024]{1,0:T(8,128)(2,1)}) %all-reduce.10.cloned.1.call-update) | async-done | bytes 2097168 | tf_op jit(solution)/shard_map/psum | solution.py:132
  241.1 13.0 %convert_reduce_fusion = (f32[2048]{0:T(1024)}, bf16[1024,2048]{1,0:T(8,128)(2,1)}) fusion(f32[1024,2048]{1,0:T(8,128)} %get-tuple-element.266, bf16[2048,1024]{1,0:T(8,128)(2,1)S(1)} %copy-done.35, f32[1024,1024]{1,0:T(8,128)S(1)} %broadcast_add_fusion.1, f32[1024,2048]{1,0:T(8,128)} %get-tuple-element.283, f32[2048]{0:T(1024)S(1)} %convert_element_type.172), kind=kOutput, calls=%fused_computation.62 | convolution fusion | flops 4331665408 | bytes 29376512 | tf_op jit(solution)/shard_map/dot_general | solution.py:28
  254.1 8.0 %convolution_convert_fusion.2 = bf16[1024,1024]{1,0:T(8,128)(2,1)} fusion(bf16[1024,2048]{1,0:T(8,128)(2,1)} %get-tuple-element.285, bf16[1024,2048]{1,0:T(8,128)(2,1)S(1)} %copy-done.37), kind=kOutput, calls=%fused_computation.118 | convolution fusion | flops 4296015872 | bytes 10485760 | tf_op jit(solution)/shard_map/dot_general | solution.py:28
  262.2 63.0 %all-reduce.12.cloned.1.call-done = bf16[1024,1024]{1,0:T(8,128)(2,1)} async-done(((bf16[1024,1024]{1,0:T(8,128)(2,1)}), bf16[1024,1024]{1,0:T(8,128)(2,1)}) %all-reduce.12.cloned.1.call-update) | async-done | bytes 2097168 | tf_op jit(solution)/shard_map/psum | solution.py:149
  325.2 5.7 multiply_reduce_fusion.1
  346.2 42.9 %while.27 = (s32[]{:T(128)}, bf16[2,512,512]{1,2,0:T(8,128)(2,1)}, bf16[2,512,512]{2,1,0:T(8,128)(2,1)}, bf16[2,512,512]{1,2,0:T(8,128)(2,1)}, bf16[2,512,8,64]{...) while((s32[]{:T(128)}, bf16[2,512,512]{1,2,0:T(8,128)(2,1)}, ...), condition=%wide.region_17.18_spmd, body=%wide.region_15.17_spmd.sunk | while | flops 1374941184 | bytes 89248512 | solution.py:160
  393.7 7.7 convert_bitcast_fusion
  401.4 7.7 copy.83
  409.1 4.8 convolution_convert_fusion.5
  414.0 10.2 %convolution_convert_fusion = bf16[2048,1024]{0,1:T(8,128)(2,1)} fusion(bf16[1024,2048]{1,0:T(8,128)(2,1)} %copy-done.40, f32[1024,1024]{1,0:T(8,128)} %copy-done.11), kind=kOutput, calls=%fused_computation.91 | convolution fusion | flops 4298113024 | bytes 12582912 | tf_op jit(solution)/shard_map/dot_general | solution.py:22
  424.3 6.6 bitcast_convert_fusion
  431.3 10.2 %convolution_convert_fusion.1 = bf16[1024,2048]{1,0:T(8,128)(2,1)} fusion(bf16[1024,2048]{1,0:T(8,128)(2,1)} %get-tuple-element.285, f32[1024,1024]{1,0:T(8,128)} %copy-done.7, f32[1024]{0:T(1024)S(1)} %copy-done.25, f32[1024]{0:T(1024)S(1)} %convert_element_type.169), kind=kOutput, calls=%fused_computation.92 | convolution fusion | flops 4300210176 | bytes 12591104 | tf_op jit(solution)/shard_map/dot_general | solution.py:22
  452.0 68.8 %all-reduce.14.cloned.1.call-done = bf16[3,1024,512]{2,0,1:T(4,128)(2,1)} async-done(((bf16[3,1024,512]{2,0,1:T(4,128)(2,1)}), bf16[3,1024,512]{2,0,1:T(4,128)(2,1)}) %all-reduce.14.cloned.1.call-update) | async-done | bytes 3145744
  522.7 57.9 %reduce-scatter.7.cloned.1.call-done = bf16[512,64]{0,1:T(8,128)(2,1)} async-done(((bf16[512,1024]{0,1:T(8,128)(2,1)}), bf16[512,64]{0,1:T(8,128)(2,1)}) %reduce-scatter.7.cloned.1.call-update) | async-done | bytes 65552 | tf_op jit(solution)/shard_map/reduce_scatter | solution.py:185
  582.1 74.2 %reduce-scatter.11.cloned.1.call-done = bf16[2048,64]{0,1:T(8,128)(2,1)} async-done(((bf16[2048,1024]{0,1:T(8,128)(2,1)}), bf16[2048,64]{0,1:T(8,128)(2,1)}) %reduce-scatter.11.cloned.1.call-update) | async-done | bytes 262160 | tf_op jit(solution)/shard_map/reduce_scatter | solution.py:191
  658.1 31.3 %reduce-scatter.5.cloned.1.call-done = bf16[512,1024]{1,0:T(8,128)(2,1)} async-done(((bf16[1024,1024]{1,0:T(8,128)(2,1)}), bf16[512,1024]{1,0:T(8,128)(2,1)}) %reduce-scatter.5.cloned.1.call-update) | async-done | bytes 1048592 | tf_op jit(solution)/shard_map/reduce_scatter | solution.py:179
  692.6 62.3 %all-reduce.1 = (f32[2,1024]{1,0:T(2,128)S(1)}, f32[1024]{0:T(1024)S(1)}, f32[1024]{0:T(1024)S(1)}, f32[1024]{0:T(1024)S(1)}, f32[4096]{0:T(1024)S(1)}, /*index=...) all-reduce(f32[2,1024]{1,0:T(2,128)S(1)} %maximum_dynamic-update-sl, ...), channel_id=1, replica_groups=mesh['dp'=16,'mp'=2] {'dp'}, use_global_device_ids=true, to_apply=%region_22.23 | all-reduce | flops 12288 | bytes 98304 | tf_op jit(solution)/shard_map/psum | solution.py:201
  754.9 8.3 %all-reduce.2 = (f32[2,1024]{1,0:T(2,128)}, f32[1024]{0:T(1024)}, f32[1024]{0:T(1024)}, f32[1024]{0:T(1024)}, f32[4096]{0:T(1024)}, /*index=5*/f32[1024]{0:T(1024)}, f32[1024]{0:T(1024)}, f32[1024]{0:T(1024)}) all-reduce(f32[2,1024]{1,0:T(2,128)S(1)} %get-tuple-element.244, ...), channel_id=1, replica_groups=mesh['dp'=16,'mp'=2] {'mp'}, use_global_device_ids=true, to_apply=%region_23.24 | all-reduce | flops 12288 | bytes 98304 | tf_op jit(solution)/shard_map/psum | solution.py:205
  (205 shorter events, 152.1 us)
Async XLA Ops:
  7.2 119.5 %all-reduce.8.cloned.1.call-start = ((), (), s32[]{:S(2)}) async-start(), calls=%async_computation.4 | async-start | bytes 4194304 | tf_op jit(solution)/shard_map/psum | solution.py:119
  56.7 4.6 copy-start.27
  60.9 167.8 %all-reduce.10.cloned.1.call-start = ((), (), s32[]{:S(2)}) async-start(), calls=%async_computation.5 | async-start | bytes 4194304 | tf_op jit(solution)/shard_map/psum | solution.py:132
  61.3 171.4 %copy-start.24 = (f32[1024]{0:T(1024)}, f32[1024]{0:T(1024)S(1)}, u32[]{:S(2)}) copy-start(f32[1024]{0:T(1024)S(1)} %convert_element_type.170) | copy-start | bytes 12292
  133.4 24.4 %copy-start.7 = (f32[1024,1024]{1,0:T(8,128)}, f32[1024,1024]{1,0:T(8,128)S(1)}, u32[]{:S(2)}) copy-start(f32[1024,1024]{1,0:T(8,128)S(1)} %broadcast_multiply_fusion) | copy-start | bytes 12582916
  133.5 26.5 %copy-start.34 = (bf16[2048,1024]{1,0:T(8,128)(2,1)S(1)}, bf16[2048,1024]{1,0:T(8,128)(2,1)}, u32[]{:S(2)}) copy-start(bf16[2048,1024]{1,0:T(8,128)(2,1)} %param.29) | copy-start | bytes 12582916
  159.9 6.2 copy-start.31
  159.9 6.2 copy-start.32
  165.7 159.5 %all-reduce.12.cloned.1.call-start = ((), (), s32[]{:S(2)}) async-start(), calls=%async_computation.6 | async-start | bytes 4194304 | tf_op jit(solution)/shard_map/psum | solution.py:149
  166.2 72.0 %copy-start.20 = (f32[1024]{0:T(1024)}, f32[1024]{0:T(1024)S(1)}, u32[]{:S(2)}) copy-start(f32[1024]{0:T(1024)S(1)} %convert_element_type.177) | copy-start | bytes 12292
  228.8 4.7 copy-start.13
  239.4 14.7 %copy-start.11 = (f32[1024,1024]{1,0:T(8,128)}, f32[1024,1024]{1,0:T(8,128)S(1)}, u32[]{:S(2)}) copy-start(f32[1024,1024]{1,0:T(8,128)S(1)} %broadcast_add_fusion.1) | copy-start | bytes 12582916
  241.1 13.0 %copy-start.37 = (bf16[1024,2048]{1,0:T(8,128)(2,1)S(1)}, bf16[1024,2048]{1,0:T(8,128)(2,1)}, u32[]{:S(2)}) copy-start(bf16[1024,2048]{1,0:T(8,128)(2,1)} %param.27) | copy-start | bytes 12582916
  262.1 258.7 %all-reduce.14.cloned.1.call-start = ((), (), s32[]{:S(2)}) async-start(), calls=%async_computation.11 | async-start | bytes 8388608
  325.2 5.8 copy-start.4
  325.2 5.8 copy-start.6
  409.1 171.5 %reduce-scatter.7.cloned.1.call-start = ((), (), s32[]{:S(2)}) async-start(), calls=%async_computation.8 | async-start | bytes 1114112 | tf_op jit(solution)/shard_map/reduce_scatter | solution.py:185
  414.0 242.3 %reduce-scatter.11.cloned.1.call-start = ((), (), s32[]{:S(2)}) async-start(), calls=%async_computation.10 | async-start | bytes 4456448 | tf_op jit(solution)/shard_map/reduce_scatter | solution.py:191
  424.3 7.0 copy-start.25
  424.3 265.1 %reduce-scatter.5.cloned.1.call-start = ((), (), s32[]{:S(2)}) async-start(), calls=%async_computation.7 | async-start | bytes 3145728 | tf_op jit(solution)/shard_map/reduce_scatter | solution.py:179
  431.0 335.8 %reduce-scatter.9.cloned.1.call-start = ((), (), s32[]{:S(2)}) async-start(), calls=%async_computation.9 | async-start | bytes 4456448 | tf_op jit(solution)/shard_map/reduce_scatter | solution.py:188
  443.4 6.0 copy-start.9
  445.8 5.8 copy-start.18
  445.8 5.8 copy-start.19
  (30 other events, 79.6 us)
Sparse Core Ops, SparseCore 0:
  61.1 65.5 all-reduce.7
  165.8 62.9 all-reduce.9
  262.2 62.9 all-reduce.11
  409.2 111.5 all-reduce.13
  524.3 56.2 reduce-scatter.6
  584.8 71.4 reduce-scatter.10
  658.5 30.8 reduce-scatter.4
  693.8 72.9 reduce-scatter.8
